TPU v7x, 32 devices: a whole 2x2x4 slice. The times are simulated.
32 devices in a mesh: view: 4 (over z), brick: 8 (over y, x, core).
Axes of the slice: x: 2, y: 2, z: 4, core: 2. Of those that a mesh axis runs over, the one named last changes fastest.
Arguments:
- estimate: float32 [16, 16, 64, 256], P('brick'), may hold values from 0.5 to 2
- views_data: bfloat16 [4, 8, 112, 32, 128], P('view', 'brick'), may hold values from 0.5 to 2
- psf_taps: float32 [4, 3, 31], P('view'), may hold values from 0.02 to 1
- seg_owner: int32 [4, 8, 32, 1], P('view', 'brick'), may hold values from 0 to 7; in each aligned block of 32 rows (0 to 31, 32 to 63, ..., all dimensions but the last counted through in order) at most 8 rows name the same one
- seg_local: int32 [4, 8, 32], P('view', 'brick'), may hold values from 0 to 1
- seg_offset: int32 [4, 8, 32], P('view', 'brick'), may hold values from 0 to 12
- seg_extent: int32 [4, 8, 32], P('view', 'brick'), may hold values from 1 to 4, 112 in all within a row
- view_shift: int32 [4, 2], P('view'), may hold values from 0 to 32
Outputs:
- joined: float32 [16, 16, 64, 256], P('brick')
Inputs may be any that keep to these rules, and one draw needn't show every extreme that they name: `seg_owner`: within one tile's 32 segments no owner is named more than 8 times, and in every draw some tile names one owner exactly 8 times. `seg_extent`: the 32 extents of a tile sum to 112, and some extent is exactly 4.
All inputs are finite; a program needn't handle non-finite values.
Results may differ from a plain program's by a relative error of at most 0.0003.
Values may be sent and summed in bfloat16 or wider, within the bound.
No kernel may reach another device: no remote copies, remote signals or barrier semaphores. Data moves between devices by JAX's collectives and lax.ppermute only.
A program may use at most 128 MiB of HBM per device.

v0:
```python
import jax
import jax.numpy as jnp
from jax import lax
from jax.sharding import PartitionSpec as P

ITERS = 2
EXTMAX = 4


def blur_matrix(tap_values, length):
    centre = tap_values.shape[0] // 2
    positions = jnp.arange(length, dtype=jnp.int32)
    offsets_tab = positions[:, None] - positions[None, :] + centre
    match_table = (
        offsets_tab[:, :, None] == jnp.arange(tap_values.shape[0], dtype=jnp.int32)[None, None, :]
    ).astype(tap_values.dtype)
    return jnp.sum(match_table * tap_values[None, None, :], axis=-1)


def apply_blur(volume, matrices):
    along_z, along_y, along_x = matrices
    highest = lax.Precision.HIGHEST
    volume = jnp.einsum("...xyz,zw->...xyw", volume, along_z, precision=highest)
    volume = jnp.einsum("...xyz,yw->...xwz", volume, along_y, precision=highest)
    volume = jnp.einsum("...xyz,xw->...wyz", volume, along_x, precision=highest)
    return volume


def view_matrices(view_taps, tile_x, tile_y, tile_z):
    normed = view_taps / jnp.sum(view_taps, axis=1, keepdims=True)
    forward = (
        blur_matrix(normed[2], tile_z),
        blur_matrix(normed[1], tile_y),
        blur_matrix(normed[0], tile_x),
    )
    backward = (forward[0].T, forward[1].T, forward[2].T)
    return (forward, backward)


def slot_ranks(owners):
    positions = jnp.arange(owners.shape[-1], dtype=jnp.int32)
    same_owner = owners[..., :, None] == owners[..., None, :]
    earlier = positions[None, :] < positions[:, None]
    return jnp.sum((same_owner & earlier).astype(jnp.int32), axis=-1)


def on_device(
    estimate, views_data, psf_taps, seg_owner, seg_local, seg_offset, seg_extent, view_shift
):
    per_owner, brick_x, brick_y, brick_z = estimate.shape
    tile_x, tile_y, tile_z = (views_data.shape[2], views_data.shape[3], views_data.shape[4])
    seg_count = seg_extent.shape[2]
    brick_count = lax.axis_size("brick")
    owner_me = lax.axis_index("brick")
    capacity = max(2, 2 * seg_count // brick_count)
    slot_rows = capacity * EXTMAX
    own_rows = per_owner * brick_x
    forward, backward = view_matrices(psf_taps[0], tile_x, tile_y, tile_z)
    shift_y = view_shift[0, 0]
    shift_z = view_shift[0, 1]
    measured = views_data[0, 0].astype(jnp.float32)
    lists = (
        lax.all_gather(seg_owner[:, :, :, 0], "brick", axis=1, tiled=True),
        lax.all_gather(seg_local, "brick", axis=1, tiled=True),
        lax.all_gather(seg_offset, "brick", axis=1, tiled=True),
        lax.all_gather(seg_extent, "brick", axis=1, tiled=True),
    )
    all_owner, all_local, all_offset, all_extent = (
        lists[0][0],
        lists[1][0],
        lists[2][0],
        lists[3][0],
    )
    own_owner = seg_owner[0, 0, :, 0]
    own_local = seg_local[0, 0]
    own_offset = seg_offset[0, 0]
    own_extent = seg_extent[0, 0]
    own_rank = slot_ranks(own_owner)
    seg_ids = jnp.arange(seg_count, dtype=jnp.int32)
    peer_ids = jnp.arange(brick_count, dtype=jnp.int32)
    slot_ids = jnp.arange(capacity, dtype=jnp.int32)
    row_steps = jnp.arange(EXTMAX, dtype=jnp.int32)
    starts = jnp.cumsum(own_extent) - own_extent
    tile_rows = jnp.arange(tile_x, dtype=jnp.int32)
    seg_of = jnp.sum((starts[None, :] <= tile_rows[:, None]).astype(jnp.int32), axis=1) - 1
    within = tile_rows - starts[seg_of]
    source_of_row = (
        (own_owner[seg_of] * per_owner + own_local[seg_of]) * brick_x + own_offset[seg_of] + within
    )
    back_match = (own_owner[None, None, :] == peer_ids[:, None, None]) & (
        own_rank[None, None, :] == slot_ids[None, :, None]
    )
    back_valid = jnp.any(back_match, axis=-1)
    back_seg = jnp.sum(back_match.astype(jnp.int32) * seg_ids, axis=-1)
    back_mask = back_valid[:, :, None] & (
        row_steps[None, None, :] < own_extent[back_seg][:, :, None]
    )
    back_rows = jnp.where(
        back_mask, starts[back_seg][:, :, None] + row_steps[None, None, :], 0
    ).reshape(-1)
    back_mask = back_mask.reshape(-1)
    all_rank = slot_ranks(all_owner)
    owner_match = (all_owner[:, None, :] == owner_me) & (
        all_rank[:, None, :] == slot_ids[None, :, None]
    )
    owner_valid = jnp.any(owner_match, axis=-1)
    owner_seg = jnp.sum(owner_match.astype(jnp.int32) * seg_ids, axis=-1)
    owner_base = jnp.take_along_axis(all_local, owner_seg, axis=1) * brick_x + jnp.take_along_axis(
        all_offset, owner_seg, axis=1
    )
    owner_ext = jnp.take_along_axis(all_extent, owner_seg, axis=1)
    owner_mask = owner_valid[:, :, None] & (row_steps[None, None, :] < owner_ext[:, :, None])
    owner_rows = jnp.where(
        owner_mask, owner_base[:, :, None] + row_steps[None, None, :], 0
    ).reshape(-1)
    owner_mask = owner_mask.reshape(-1)
    landing = (
        (owner_rows[None, :] == jnp.arange(own_rows, dtype=jnp.int32)[:, None])
        & owner_mask[None, :]
    ).astype(jnp.float32)

    def to_owners(projected):
        outgoing = jnp.where(back_mask[:, None, None], jnp.take(projected, back_rows, axis=0), 0.0)
        outgoing = outgoing.reshape(brick_count, slot_rows, tile_y, tile_z)
        arrived = lax.all_to_all(
            outgoing, "brick", split_axis=0, concat_axis=0, tiled=True
        ).reshape(-1, tile_y, tile_z)
        accumulated = jnp.einsum("pq,qyz->pyz", landing, arrived, precision=lax.Precision.HIGHEST)
        brick_part = lax.dynamic_update_slice(
            jnp.zeros((own_rows, brick_y, brick_z), jnp.float32), accumulated, (0, shift_y, shift_z)
        )
        brick_part = brick_part.reshape(per_owner, brick_x, brick_y, brick_z)
        return lax.psum(brick_part, "view")

    weight = to_owners(apply_blur(jnp.ones((tile_x, tile_y, tile_z), jnp.float32), backward))
    current = estimate
    for sweep in range(ITERS):
        flat_est = current.reshape(own_rows, brick_y, brick_z)
        cropped = lax.dynamic_slice(
            flat_est, (0, shift_y, shift_z), (own_rows, tile_y, tile_z)
        ).astype(jnp.bfloat16)
        gathered = lax.all_gather(cropped, "brick", axis=0, tiled=True)
        view_tile = jnp.take(gathered, source_of_row, axis=0)
        correction_view_tile = view_tile.astype(jnp.float32)
        quotient = measured / apply_blur(correction_view_tile, forward)
        correction = to_owners(apply_blur(quotient, backward))
        current = current * (1.0 + correction) / (1.0 + weight)
    return current


def solution(mesh):
    placed = (
        P("brick", None, None, None),
        P("view", "brick", None, None, None),
        P("view", None, None),
        P("view", "brick", None, None),
        P("view", "brick", None),
        P("view", "brick", None),
        P("view", "brick", None),
        P("view", None),
    )
    return jax.shard_map(
        on_device,
        mesh=mesh,
        in_specs=placed,
        out_specs=P("brick", None, None, None),
        check_vma=False,
    )
```

profile of v0, /device:TPU:0, one launch (start us, length us, event | category | flops | bytes accessed | tf_op | source)
XLA Modules:
  0.0 637.1 jit_solution(17363092485871562912)
XLA Ops:
  11.9 2.2 dynamic-slice_convert_fusion.1
  17.0 1.6 gather_fusion.1
  25.0 1.6 fusion.22
  26.6 1.7 convolution_bitcast_fusion.2
  28.3 2.6 fusion.6
  31.5 3.0 gather_fusion.11
  34.6 10.2 %all-gather.4.cloned.1.call-done = bf16[256,32,128]{2,1,0:T(8,128)(2,1)} async-done(((bf16[32,32,128]{2,1,0:T(8,128)(2,1)}), bf16[256,32,128]{2,1,0:T(8,128)(2,1)}) %all-gather.4.cloned.1.call-update) | async-done | bytes 2097168 | tf_op jit(solution)/shard_map/all_gather | solution.py:142
  44.8 2.3 gather_fusion.9
  48.1 1.7 convolution_bitcast_fusion.4
  49.8 3.1 convert_divide_fusion.1
  52.9 2.0 fusion.10
  54.9 1.7 convolution_bitcast_fusion.3
  56.6 2.6 fusion.8
  59.9 3.0 gather_fusion.10
  62.8 16.0 %select_select_fusion.1 = (f32[256,32,128]{2,1,0:T(8,128)S(1)}, f32[256,32,128]{2,1,0:T(8,128)}) fusion(f32[256,32,128]{2,1,0:T(8,128)} %gather_fusion.11, pred[256]{0:T(512)(128)(4,1)S(1)} %get-tuple-element.12, pred[256]{0:T(512)(128)(4,1)S(1)} %and.102, f32[256,32,128]{2,1,0:T(8,128)} %gather_fusion.10), kind=kLoop, calls=%fused_computation.15 | loop fusion | flops 4194304 | bytes 16777728 | tf_op jit(solution)/shard_map/jit(_where)/select_n | solution.py:123
  78.8 4.3 copy.69
  83.2 4.5 all-to-all-start.1
  87.7 6.5 %copy.64 = f32[8,32,32,128]{3,1,2,0:T(8,128)} copy(f32[8,32,32,128]{3,2,1,0:T(8,128)} %bitcast.133) | data formatting | bytes 8388608 | tf_op jit(solution)/shard_map/reshape | solution.py:124
  94.3 42.6 %all-to-all-done.1 = f32[8,32,32,128]{3,1,2,0:T(8,128)} async-done(((f32[8,32,32,128]{3,1,2,0:T(8,128)}), f32[8,32,32,128]{3,1,2,0:T(8,128)}, u32[]{:S(2)}, u32[]{:S(2)}) %all-to-all-start.1) | async-done | bytes 4194336 | tf_op jit(solution)/shard_map/all_to_all | solution.py:125
  136.8 4.6 all-to-all-start
  141.5 52.0 %all-gather = s32[1,8,32,1]{2,3,0,1:T(1,128)S(1)} all-gather(s32[1,1,32,1]{2,3,0,1:T(1,128)S(1)} %bitcast.124), channel_id=2, replica_groups=mesh['view'=4,'brick'=8] {'brick'}, dimensions={1}, use_global_device_ids=true | all-gather | bytes 1152 | tf_op jit(solution)/shard_map/all_gather | solution.py:63
  194.1 7.9 %all_gather.20 = s32[1,8,32]{2,0,1:T(1,128)S(1)} all-gather(s32[1,1,32]{2,0,1:T(1,128)S(1)} %bitcast.126), channel_id=1, replica_groups=mesh['view'=4,'brick'=8] {'brick'}, dimensions={1}, use_global_device_ids=true | all-gather | bytes 1152 | tf_op jit(solution)/shard_map/all_gather | solution.py:64
  202.8 8.7 %all_gather.21 = s32[1,8,32]{2,0,1:T(1,128)S(1)} all-gather(s32[1,1,32]{2,0,1:T(1,128)S(1)} %bitcast.128), channel_id=1, replica_groups=mesh['view'=4,'brick'=8] {'brick'}, dimensions={1}, use_global_device_ids=true | all-gather | bytes 1152 | tf_op jit(solution)/shard_map/all_gather | solution.py:65
  212.3 7.9 %all_gather.19 = s32[1,8,32]{2,0,1:T(1,128)S(1)} all-gather(s32[1,1,32]{2,0,1:T(1,128)S(1)} %bitcast.117), channel_id=1, replica_groups=mesh['view'=4,'brick'=8] {'brick'}, dimensions={1}, use_global_device_ids=true | all-gather | bytes 1152 | tf_op jit(solution)/shard_map/all_gather | solution.py:66
  221.6 2.8 copy.70
  224.5 1.6 fusion.47
  226.5 2.8 copy.65
  229.3 1.6 fusion.49
  231.5 13.4 %dynamic_update_slice.10 = f32[32,64,256]{2,1,0:T(8,128)S(1)} dynamic-update-slice(f32[32,64,256]{2,1,0:T(8,128)S(1)} %broadcast.183.clone.1, f32[32,32,128]{2,1,0:T(8,128)S(1)} %copy.71, s32[]{:T(128)} %constant.39.clone.1, s32[]{:T(128)S(6)} %select_n.82, s32[]{:T(128)S(6)} %select_n.83) | dynamic-update-slice | bytes 1048580 | tf_op jit(solution)/shard_map/dynamic_update_slice | solution.py:129
  244.9 1.7 broadcast.183.clone
  246.6 13.9 %dynamic_update_slice.9 = f32[32,64,256]{2,1,0:T(8,128)} dynamic-update-slice(f32[32,64,256]{2,1,0:T(8,128)} %broadcast.183.clone, f32[32,32,128]{2,1,0:T(8,128)S(1)} %copy.66, s32[]{:T(128)} %constant.39.clone.1, s32[]{:T(128)S(6)} %select_n.82, s32[]{:T(128)S(6)} %select_n.83) | dynamic-update-slice | bytes 1048580 | tf_op jit(solution)/shard_map/dynamic_update_slice | solution.py:129
  260.6 154.2 %all-reduce.6.cloned.1.call-done = (f32[2,16,64,256]{3,2,1,0:T(8,128)}, f32[2,16,64,256]{3,2,1,0:T(8,128)}) async-done(((f32[2,16,64,256]{3,2,1,0:T(8,128)}, f32[2,16,64,256]{3,2,1,0:T(8,128)}), (f32[2,16,64,256]{3,2,1,0:T(8,128)}, f32[2,16,64,256]{3,2,1,0:T(8,128)})) %all-reduce.6.cloned.1.call-update) | async-done | bytes 4194320 | tf_op jit(solution)/shard_map/psum | solution.py:133
  414.8 3.5 multiply_divide_fusion.1
  420.7 26.6 %all-gather.6.cloned.1.call-done = bf16[256,32,128]{2,1,0:T(8,128)(2,1)} async-done(((bf16[32,32,128]{2,1,0:T(8,128)(2,1)}), bf16[256,32,128]{2,1,0:T(8,128)(2,1)}) %all-gather.6.cloned.1.call-update) | async-done | bytes 2097168 | tf_op jit(solution)/shard_map/all_gather | solution.py:142
  447.4 2.3 gather_fusion.12
  450.7 1.7 convolution_bitcast_fusion.1
  452.4 2.9 convert_divide_fusion
  455.3 2.0 fusion.2
  457.3 1.7 convolution_bitcast_fusion
  459.0 2.9 fusion
  462.5 3.0 gather_fusion.13
  465.5 3.8 select_select_fusion
  469.2 2.4 copy.78
  471.6 51.6 %all_to_all.15 = f32[8,32,32,128]{3,1,2,0:T(8,128)S(1)} all-to-all(f32[8,32,32,128]{3,1,2,0:T(8,128)S(1)} %copy.78), channel_id=1, replica_groups=mesh['view'=4,'brick'=8] {'brick'}, dimensions={0} | all-to-all | bytes 8388608 | tf_op jit(solution)/shard_map/all_to_all | solution.py:125
  523.8 1.6 fusion.45
  527.3 14.1 %dynamic_update_slice.11 = f32[32,64,256]{2,1,0:T(8,128)} dynamic-update-slice(f32[32,64,256]{2,1,0:T(8,128)} %broadcast.183, f32[32,32,128]{2,1,0:T(8,128)S(1)} %copy.80, s32[]{:T(128)} %constant.39.clone.1, s32[]{:T(128)S(6)} %select_n.82, s32[]{:T(128)S(6)} %select_n.83) | dynamic-update-slice | bytes 1048580 | tf_op jit(solution)/shard_map/dynamic_update_slice | solution.py:129
  541.4 84.5 %all-reduce.4.cloned.1.call-done = f32[2,16,64,256]{3,2,1,0:T(8,128)} async-done(((f32[2,16,64,256]{3,2,1,0:T(8,128)}), f32[2,16,64,256]{3,2,1,0:T(8,128)}) %all-reduce.4.cloned.1.call-update) | async-done | bytes 2097168 | tf_op jit(solution)/shard_map/psum | solution.py:133
  625.9 4.2 multiply_divide_fusion
  (101 shorter events, 23.8 us)
Async XLA Ops:
  6.5 12.1 %copy-start.1 = (s32[1,1,32,1]{2,3,1,0:T(1,128)S(1)}, s32[1,1,32,1]{2,3,1,0:T(1,128)}, u32[]{:S(2)}) copy-start(s32[1,1,32,1]{2,3,1,0:T(1,128)} %param.17) | copy-start | bytes 388
  6.5 12.3 %copy-start.2 = (s32[1,1,32]{2,1,0:T(1,128)S(1)}, s32[1,1,32]{2,1,0:T(1,128)}, u32[]{:S(2)}) copy-start(s32[1,1,32]{2,1,0:T(1,128)} %param.18) | copy-start | bytes 388
  6.5 13.5 %copy-start.3 = (s32[1,1,32]{2,1,0:T(1,128)S(1)}, s32[1,1,32]{2,1,0:T(1,128)}, u32[]{:S(2)}) copy-start(s32[1,1,32]{2,1,0:T(1,128)} %param.19) | copy-start | bytes 388
  6.5 38.2 %all-gather.4.cloned.1.call-start = ((), (), s32[]{:S(2)}) async-start(), calls=%async_computation.3 | async-start | bytes 2359296 | tf_op jit(solution)/shard_map/all_gather | solution.py:142
  21.6 0.8 copy-start
  22.4 1.6 copy-start.7
  48.1 1.7 copy-start.8
  83.2 53.6 %all-to-all-start.1 = ((f32[8,32,32,128]{3,1,2,0:T(8,128)}), f32[8,32,32,128]{3,1,2,0:T(8,128)}, u32[]{:S(2)}, u32[]{:S(2)}) async-start(f32[8,32,32,128]{3,1,2,0:T(8,128)} %copy.69), calls=%async_computation.1 | async-start | bytes 8388608 | tf_op jit(solution)/shard_map/all_to_all | solution.py:125
  136.8 89.6 %all-to-all-start = ((f32[8,32,32,128]{3,1,2,0:T(8,128)}), f32[8,32,32,128]{3,1,2,0:T(8,128)}, u32[]{:S(2)}, u32[]{:S(2)}) async-start(f32[8,32,32,128]{3,1,2,0:T(8,128)} %copy.64), calls=%async_computation | async-start | bytes 8388608 | tf_op jit(solution)/shard_map/all_to_all | solution.py:125
  141.4 273.3 %all-reduce.6.cloned.1.call-start = ((), (), s32[]{:S(2)}) async-start(), calls=%async_computation.6 | async-start | bytes 8388608 | tf_op jit(solution)/shard_map/psum | solution.py:133
  244.9 15.6 %copy-start.6 = (f32[32,64,256]{2,1,0:T(8,128)}, f32[32,64,256]{2,1,0:T(8,128)S(1)}, u32[]{:S(2)}) copy-start(f32[32,64,256]{2,1,0:T(8,128)S(1)} %dynamic_update_slice.10) | copy-start | bytes 6291460
  260.5 186.9 %all-gather.6.cloned.1.call-start = ((), (), s32[]{:S(2)}) async-start(), calls=%async_computation.4 | async-start | bytes 2359296 | tf_op jit(solution)/shard_map/all_gather | solution.py:142
  418.2 1.3 copy-start.4
  420.5 205.4 %all-reduce.4.cloned.1.call-start = ((), (), s32[]{:S(2)}) async-start(), calls=%async_computation.5 | async-start | bytes 4194304 | tf_op jit(solution)/shard_map/psum | solution.py:133
  450.7 1.7 copy-start.9
  527.3 98.5 %copy-start.5 = (f32[2,16,64,256]{3,2,1,0:T(8,128)S(1)}, f32[2,16,64,256]{3,2,1,0:T(8,128)}, u32[]{:S(2)}) copy-start(f32[2,16,64,256]{3,2,1,0:T(8,128)} %copy-done.4) | copy-start | bytes 6291460
Sparse Core Ops, SparseCore 0:
  14.2 30.5 all-gather.3
  260.6 154.0 all-reduce.5
  420.6 26.7 all-gather.5
  541.5 84.2 all-reduce.3
where the time goes:
time: 648 us; the launch traced here: 637 us
  waiting for transfers between devices  318 us (49%)
  blocking collectives  128 us (20%)
  local copies, waits for them, and re-layouts  97.2 us (15%)
  matrix products  35 us (5%)
  other arithmetic  31.1 us (5%)
  between operations  18.1 us (3%)
  starting transfers between devices  9.48 us (1%)
    psum x2, waiting for transfers between devices, to_owners(): return lax.psum(brick_part, 'view')  239 us
    all_gather x1, blocking collectives, on_device(): lax.all_gather(seg_owner[:, :, :, 0], 'brick', axis=1, tiled=True)  52 us
    all_to_all x1, blocking collectives, to_owners(): lax.all_to_all(outgoing, 'brick', split_axis=0, concat_axis=0, tiled=True)  51.6 us
    all_to_all x2, waiting for transfers between devices, to_owners(): lax.all_to_all(outgoing, 'brick', split_axis=0, concat_axis=0, tiled=True)  42.6 us
    dynamic_update_slice x3, local copies, waits for them, and re-layouts, to_owners(): lax.dynamic_update_slice(jnp.zeros((own_rows, brick_y, brick_z), jnp.floa...  41.3 us
    all_gather x2, waiting for transfers between devices, on_device(): gathered = lax.all_gather(cropped, 'brick', axis=0, tiled=True)  36.9 us
    select_n x2, other arithmetic, to_owners(): jnp.where(back_mask[:, None, None], jnp.take(projected, back_rows, axis=0...  19.7 us
    dot_general x5, matrix products, apply_blur(): volume = jnp.einsum('...xyz,xw->...wyz', volume, along_x, precision=highest)  14.2 us
  transfers between devices with their start and end apart: 6, of which 5 were waited for; matrix products, arithmetic and copies ran while one was open for 6% of the time, Pallas kernels for 0%

commit v1 on v0

--- a/solution.py
+++ b/solution.py
@@ -5,6 +5,23 @@
 
 ITERS = 2
 EXTMAX = 4
+
+
+def laid_out(pieces, dim):
+    shape = list(pieces.shape[1:])
+    shape[dim] *= pieces.shape[0]
+    return jnp.moveaxis(pieces, 0, dim).reshape(shape)
+
+
+def ring_gather(value, axis, dim):
+    size = lax.axis_size(axis)
+    upward = [(i, (i + 1) % size) for i in range(size)]
+    blocks = [value]
+    while len(blocks) < size:
+        blocks.append(lax.ppermute(blocks[-1], axis, upward))
+    mine = lax.axis_index(axis)
+    blocks = jnp.stack(blocks)[(mine - jnp.arange(size)) % size]
+    return laid_out(blocks, dim)
 
 
 def blur_matrix(tap_values, length):
@@ -139,7 +156,7 @@
         cropped = lax.dynamic_slice(
             flat_est, (0, shift_y, shift_z), (own_rows, tile_y, tile_z)
         ).astype(jnp.bfloat16)
-        gathered = lax.all_gather(cropped, "brick", axis=0, tiled=True)
+        gathered = ring_gather(cropped, "brick", 0)
         view_tile = jnp.take(gathered, source_of_row, axis=0)
         correction_view_tile = view_tile.astype(jnp.float32)
         quotient = measured / apply_blur(correction_view_tile, forward)

time: 648 us -> 685 us (1.057)
  waiting for transfers between devices: 318 us -> 347 us
  local copies, waits for them, and re-layouts: 97.2 us -> 111 us
  other arithmetic: 31.1 us -> 22.3 us
    ppermute x0 -> x14, waiting for transfers between devices: none -> 65.6 us  [ring_gather(): blocks.append(lax.ppermute(blocks[-1], axis, upward))]
    all_gather x2 -> x0, waiting for transfers between devices: 36.9 us -> none  [on_device(): gathered = lax.all_gather(cropped, 'brick', axis=0, tiled=True)]
    unnamed x20 -> x36, local copies, waits for them, and re-layouts: 1.35 us -> 13.1 us
    select_n x2, other arithmetic: 19.7 us -> 9.59 us  [to_owners(): jnp.where(back_mask[:, None, None], jnp.take(projected, back_rows, axis=0...]
  transfers between devices with their start and end apart: 6 -> 18, of which waited for: 5 -> 16; matrix products, arithmetic and copies ran while one was open for 6% -> 7% of each run, Pallas kernels for 0% -> 0%
where the time goes in v1:
time: 685 us; the launch traced here: 676 us
  waiting for transfers between devices  347 us (51%)
  blocking collectives  128 us (19%)
  local copies, waits for them, and re-layouts  111 us (16%)
  matrix products  36.3 us (5%)
  other arithmetic  22.3 us (3%)
  between operations  18.3 us (3%)
  starting transfers between devices  12.8 us (2%)
    psum x2, waiting for transfers between devices, to_owners(): return lax.psum(brick_part, 'view')  239 us
    ppermute x14, waiting for transfers between devices, ring_gather(): blocks.append(lax.ppermute(blocks[-1], axis, upward))  65.6 us
    all_gather x1, blocking collectives, on_device(): lax.all_gather(seg_owner[:, :, :, 0], 'brick', axis=1, tiled=True)  52 us
    all_to_all x1, blocking collectives, to_owners(): lax.all_to_all(outgoing, 'brick', split_axis=0, concat_axis=0, tiled=True)  51.6 us
    all_to_all x2, waiting for transfers between devices, to_owners(): lax.all_to_all(outgoing, 'brick', split_axis=0, concat_axis=0, tiled=True)  42.6 us
    dynamic_update_slice x3, local copies, waits for them, and re-layouts, to_owners(): lax.dynamic_update_slice(jnp.zeros((own_rows, brick_y, brick_z), jnp.floa...  41.4 us
    dot_general x5, matrix products, apply_blur(): volume = jnp.einsum('...xyz,xw->...wyz', volume, along_x, precision=highest)  15.6 us
  transfers between devices with their start and end apart: 18, of which 16 were waited for; matrix products, arithmetic and copies ran while one was open for 7% of the time, Pallas kernels for 0%

profile of v1, /device:TPU:0, one launch (start us, length us, event | category | flops | bytes accessed | tf_op | source)
XLA Modules:
  0.0 675.6 jit_solution(17289332795131788567)
XLA Ops:
  11.7 2.2 bitcast_dynamic-update-slice_fusion.15
  23.3 3.9 fusion.6
  28.3 2.6 collective-permute-start.1
  31.1 4.1 collective-permute-done.1
  42.0 2.1 copy.68
  44.0 3.0 gather_fusion.13
  50.1 5.3 collective-permute-done.4
  56.8 5.3 collective-permute-done.5
  63.7 5.2 collective-permute-done.6
  69.6 2.5 gather_fusion.1
  75.6 2.9 convert_divide_fusion.1
  78.5 2.0 fusion.10
  82.1 3.0 fusion.8
  85.8 3.0 gather_fusion.12
  88.7 5.8 select_select_fusion.1
  94.5 4.3 copy.69
  98.9 4.5 all-to-all-start.1
  103.4 6.5 copy.64
  109.9 42.6 %all-to-all-done.1 = f32[8,32,32,128]{3,1,2,0:T(8,128)} async-done(((f32[8,32,32,128]{3,1,2,0:T(8,128)}), f32[8,32,32,128]{3,1,2,0:T(8,128)}, u32[]{:S(2)}, u32[]{:S(2)}) %all-to-all-start.1) | async-done | bytes 4194336 | tf_op jit(solution)/shard_map/all_to_all | solution.py:142
  152.5 4.6 all-to-all-start
  157.2 52.0 %all-gather = s32[1,8,32,1]{2,3,0,1:T(1,128)S(1)} all-gather(s32[1,1,32,1]{2,3,0,1:T(1,128)S(1)} %bitcast.160), channel_id=2, replica_groups=mesh['view'=4,'brick'=8] {'brick'}, dimensions={1}, use_global_device_ids=true | all-gather | bytes 1152 | tf_op jit(solution)/shard_map/all_gather | solution.py:80
  209.8 7.9 %all_gather.14 = s32[1,8,32]{2,0,1:T(1,128)S(1)} all-gather(s32[1,1,32]{2,0,1:T(1,128)S(1)} %bitcast.162), channel_id=1, replica_groups=mesh['view'=4,'brick'=8] {'brick'}, dimensions={1}, use_global_device_ids=true | all-gather | bytes 1152 | tf_op jit(solution)/shard_map/all_gather | solution.py:81
  218.5 8.7 %all_gather.15 = s32[1,8,32]{2,0,1:T(1,128)S(1)} all-gather(s32[1,1,32]{2,0,1:T(1,128)S(1)} %bitcast.164), channel_id=1, replica_groups=mesh['view'=4,'brick'=8] {'brick'}, dimensions={1}, use_global_device_ids=true | all-gather | bytes 1152 | tf_op jit(solution)/shard_map/all_gather | solution.py:82
  228.0 8.1 %all_gather.13 = s32[1,8,32]{2,0,1:T(1,128)S(1)} all-gather(s32[1,1,32]{2,0,1:T(1,128)S(1)} %bitcast.153), channel_id=1, replica_groups=mesh['view'=4,'brick'=8] {'brick'}, dimensions={1}, use_global_device_ids=true | all-gather | bytes 1152 | tf_op jit(solution)/shard_map/all_gather | solution.py:83
  237.5 2.8 copy.70
  242.3 2.8 copy.65
  248.1 13.4 %dynamic_update_slice.10 = f32[32,64,256]{2,1,0:T(8,128)S(1)} dynamic-update-slice(f32[32,64,256]{2,1,0:T(8,128)S(1)} %broadcast.247.clone.1, f32[32,32,128]{2,1,0:T(8,128)S(1)} %copy.71, s32[]{:T(128)} %constant.42.clone.1, s32[]{:T(128)S(6)} %select_n.109, s32[]{:T(128)S(6)} %select_n.110) | dynamic-update-slice | bytes 1048580 | tf_op jit(solution)/shard_map/dynamic_update_slice | solution.py:146
  263.1 13.9 %dynamic_update_slice.9 = f32[32,64,256]{2,1,0:T(8,128)} dynamic-update-slice(f32[32,64,256]{2,1,0:T(8,128)} %broadcast.247.clone, f32[32,32,128]{2,1,0:T(8,128)S(1)} %copy-done.7, s32[]{:T(128)} %constant.42.clone.1, s32[]{:T(128)S(6)} %select_n.109, s32[]{:T(128)S(6)} %select_n.110) | dynamic-update-slice | bytes 1048580 | tf_op jit(solution)/shard_map/dynamic_update_slice | solution.py:146
  277.1 155.1 %all-reduce.6.cloned.1.call-done = (f32[2,16,64,256]{3,2,1,0:T(8,128)}, f32[2,16,64,256]{3,2,1,0:T(8,128)}) async-done(((f32[2,16,64,256]{3,2,1,0:T(8,128)}, f32[2,16,64,256]{3,2,1,0:T(8,128)}), (f32[2,16,64,256]{3,2,1,0:T(8,128)}, f32[2,16,64,256]{3,2,1,0:T(8,128)})) %all-reduce.6.cloned.1.call-update) | async-done | bytes 4194320 | tf_op jit(solution)/shard_map/psum | solution.py:150
  432.2 3.5 multiply_divide_fusion.1
  437.9 6.7 collective-permute-done.7
  444.6 6.7 collective-permute-done.8
  451.3 6.7 collective-permute-done.9
  458.0 6.7 collective-permute-done.10
  466.1 5.3 collective-permute-done.11
  472.8 5.2 collective-permute-done.12
  479.7 5.2 collective-permute-done.13
  485.6 2.5 gather_fusion.7
  491.6 2.9 convert_divide_fusion
  494.5 2.0 fusion.2
  498.1 2.9 fusion
  501.6 3.0 gather_fusion.15
  504.6 3.8 select_select_fusion
  508.4 2.4 copy.78
  510.8 51.6 %all_to_all.15 = f32[8,32,32,128]{3,1,2,0:T(8,128)S(1)} all-to-all(f32[8,32,32,128]{3,1,2,0:T(8,128)S(1)} %copy.78), channel_id=1, replica_groups=mesh['view'=4,'brick'=8] {'brick'}, dimensions={0} | all-to-all | bytes 8388608 | tf_op jit(solution)/shard_map/all_to_all | solution.py:142
  566.5 14.1 %dynamic_update_slice.11 = f32[32,64,256]{2,1,0:T(8,128)} dynamic-update-slice(f32[32,64,256]{2,1,0:T(8,128)} %broadcast.247, f32[32,32,128]{2,1,0:T(8,128)S(1)} %copy.80, s32[]{:T(128)} %constant.42.clone.1, s32[]{:T(128)S(6)} %select_n.109, s32[]{:T(128)S(6)} %select_n.110) | dynamic-update-slice | bytes 1048580 | tf_op jit(solution)/shard_map/dynamic_update_slice | solution.py:146
  580.6 83.5 %all-reduce.4.cloned.1.call-done = f32[2,16,64,256]{3,2,1,0:T(8,128)} async-done(((f32[2,16,64,256]{3,2,1,0:T(8,128)}), f32[2,16,64,256]{3,2,1,0:T(8,128)}) %all-reduce.4.cloned.1.call-update) | async-done | bytes 2097168 | tf_op jit(solution)/shard_map/psum | solution.py:150
  664.1 4.2 multiply_divide_fusion
  (142 shorter events, 58.4 us)
Async XLA Ops:
  6.5 11.6 %copy-start = (s32[1,1,32]{2,1,0:T(1,128)S(1)}, s32[1,1,32]{2,1,0:T(1,128)}, u32[]{:S(2)}) copy-start(s32[1,1,32]{2,1,0:T(1,128)} %param.20) | copy-start | bytes 388
  13.9 14.3 %collective-permute-start = (bf16[32,32,128]{2,1,0:T(8,128)(2,1)S(1)}, bf16[32,32,128]{2,1,0:T(8,128)(2,1)S(1)}, u32[]{:S(2)}, u32[]{:S(2)}) collective-permute-start(bf16[32,32,128]{2,1,0:T(8,128)(2,1)S(1)} %get-tuple-element.19), channel_id=1, source_target_pairs={{0,1},{1,2},{2,3},{3,4},{4,5},{5,6},{6,7},{7,0},{8,9},{9,10},{10,1... | collective-permute-start | bytes 786440 | tf_op jit(solution)/shard_map/ppermute | solution.py:21
  18.2 0.9 copy-start.8
  27.3 9.2 %copy-start.1 = (s32[1,1,32,1]{2,3,1,0:T(1,128)S(1)}, s32[1,1,32,1]{2,3,1,0:T(1,128)}, u32[]{:S(2)}) copy-start(s32[1,1,32,1]{2,3,1,0:T(1,128)} %param.17) | copy-start | bytes 388
  27.3 10.4 %copy-start.2 = (s32[1,1,32]{2,1,0:T(1,128)S(1)}, s32[1,1,32]{2,1,0:T(1,128)}, u32[]{:S(2)}) copy-start(s32[1,1,32]{2,1,0:T(1,128)} %param.18) | copy-start | bytes 388
  27.3 11.7 %copy-start.3 = (s32[1,1,32]{2,1,0:T(1,128)S(1)}, s32[1,1,32]{2,1,0:T(1,128)}, u32[]{:S(2)}) copy-start(s32[1,1,32]{2,1,0:T(1,128)} %param.19) | copy-start | bytes 388
  28.3 7.0 %collective-permute-start.1 = (bf16[32,32,128]{2,1,0:T(8,128)(2,1)S(1)}, bf16[32,32,128]{2,1,0:T(8,128)(2,1)S(1)}, u32[]{:S(2)}, u32[]{:S(2)}) collective-permute-start(bf16[32,32,128]{2,1,0:T(8,128)(2,1)S(1)} %collective-permute-done), channel_id=1, source_target_pairs={{0,1},{1,2},{2,3},{3,4},{4,5},{5,6},{6,7},{7,0},{8,9},{9,10},{10,1... | collective-permute-start | bytes 786440 | tf_op jit(solution)/shard_map/ppermute | solution.py:21
  35.2 6.7 collective-permute-start.2
  41.9 6.7 collective-permute-start.3
  48.6 6.7 collective-permute-start.4
  55.3 6.7 collective-permute-start.5
  62.0 6.9 %collective-permute-start.6 = (bf16[32,32,128]{2,1,0:T(8,128)(2,1)S(1)}, bf16[32,32,128]{2,1,0:T(8,128)(2,1)S(1)}, u32[]{:S(2)}, u32[]{:S(2)}) collective-permute-start(bf16[32,32,128]{2,1,0:T(8,128)(2,1)S(1)} %collective-permute-done.5), channel_id=1, source_target_pairs={{0,1},{1,2},{2,3},{3,4},{4,5},{5,6},{6,7},{7,0},{8,9},{9,10},{10,1... | collective-permute-start | bytes 786440 | tf_op jit(solution)/shard_map/ppermute | solution.py:21
  73.9 1.7 copy-start.9
  98.9 53.6 %all-to-all-start.1 = ((f32[8,32,32,128]{3,1,2,0:T(8,128)}), f32[8,32,32,128]{3,1,2,0:T(8,128)}, u32[]{:S(2)}, u32[]{:S(2)}) async-start(f32[8,32,32,128]{3,1,2,0:T(8,128)} %copy.69), calls=%async_computation.1 | async-start | bytes 8388608 | tf_op jit(solution)/shard_map/all_to_all | solution.py:142
  152.5 89.8 %all-to-all-start = ((f32[8,32,32,128]{3,1,2,0:T(8,128)}), f32[8,32,32,128]{3,1,2,0:T(8,128)}, u32[]{:S(2)}, u32[]{:S(2)}) async-start(f32[8,32,32,128]{3,1,2,0:T(8,128)} %copy.64), calls=%async_computation | async-start | bytes 8388608 | tf_op jit(solution)/shard_map/all_to_all | solution.py:142
  157.1 275.1 %all-reduce.6.cloned.1.call-start = ((), (), s32[]{:S(2)}) async-start(), calls=%async_computation.4 | async-start | bytes 8388608 | tf_op jit(solution)/shard_map/psum | solution.py:150
  261.5 15.5 %copy-start.6 = (f32[32,64,256]{2,1,0:T(8,128)}, f32[32,64,256]{2,1,0:T(8,128)S(1)}, u32[]{:S(2)}) copy-start(f32[32,64,256]{2,1,0:T(8,128)S(1)} %dynamic_update_slice.10) | copy-start | bytes 6291460
  261.5 1.6 copy-start.7
  277.0 387.1 %all-reduce.4.cloned.1.call-start = ((), (), s32[]{:S(2)}) async-start(), calls=%async_computation.3 | async-start | bytes 4194304 | tf_op jit(solution)/shard_map/psum | solution.py:150
  435.7 1.3 copy-start.4
  437.9 6.7 collective-permute-start.7
  444.6 6.7 collective-permute-start.8
  451.3 6.7 collective-permute-start.9
  457.9 6.7 collective-permute-start.10
  464.6 6.7 collective-permute-start.11
  471.3 6.7 collective-permute-start.12
  478.0 6.9 %collective-permute-start.13 = (bf16[32,32,128]{2,1,0:T(8,128)(2,1)S(1)}, bf16[32,32,128]{2,1,0:T(8,128)(2,1)S(1)}, u32[]{:S(2)}, u32[]{:S(2)}) collective-permute-start(bf16[32,32,128]{2,1,0:T(8,128)(2,1)S(1)} %collective-permute-done.12), channel_id=1, source_target_pairs={{0,1},{1,2},{2,3},{3,4},{4,5},{5,6},{6,7},{7,0},{8,9},{9,10},{10,1... | collective-permute-start | bytes 786440 | tf_op jit(solution)/shard_map/ppermute | solution.py:21
  489.9 1.7 copy-start.10
  566.5 97.6 %copy-start.5 = (f32[2,16,64,256]{3,2,1,0:T(8,128)S(1)}, f32[2,16,64,256]{3,2,1,0:T(8,128)}, u32[]{:S(2)}) copy-start(f32[2,16,64,256]{3,2,1,0:T(8,128)} %copy-done.4) | copy-start | bytes 6291460
Sparse Core Ops, SparseCore 0:
  277.2 154.9 all-reduce.5
  580.8 83.2 all-reduce.3
